TPU v7x, 32 devices: a whole 2x2x4 slice. The times are simulated.
32 devices in a mesh: mode: 8 (over y, x, core), rows: 4 (over z).
Axes of the slice: x: 2, y: 2, z: 4, core: 2. Of those that a mesh axis runs over, the one named last changes fastest.
Arguments:
- tangents: float32 [128, 3, 32, 1024], P('mode', None, 'rows'), may hold values from -6 to 6
- checkpoints: float32 [8, 3, 32, 1024], P(None, None, 'rows', 'mode'), may hold values from 0 to 0.5
- owner_order: int32 [8], replicated, may hold values from 0 to 7, each once
- land_mask: int32 [32, 1024], P('rows'), may hold values 0 or 1
- coefficients: float32 [128, 128], replicated, may hold values from -0.9 to 0.9
Outputs:
- vectors: float32 [128, 3, 32, 1024], P(None, None, 'rows', 'mode')
Inputs may be any that keep to these rules, and one draw needn't show every extreme that they name: `owner_order`: every checkpoint slot is named by exactly one step.
All inputs are finite; a program needn't handle non-finite values. No bound on the sum of `land_mask` on one device may be relied on, other than what follows from the above.
Results may differ from a plain program's by a relative error of at most 0.0002.
Values sent between devices are 32-bit elements; how exact they have to be, the bound alone decides.
A program may use at most 64 MiB of HBM per device.

v0:
```python
import jax
import jax.numpy as jnp
from jax import lax
from jax.sharding import PartitionSpec as P

mean_depth = 1.0
gravity = 1.0
coriolis = 0.5
time_step = 0.5


def padded(cells, sides, width):
    for axis, dim in sides:
        count = lax.axis_size(axis)
        ends = count - 1
        head = lax.slice_in_dim(cells, 0, width, axis=dim)
        tail = lax.slice_in_dim(cells, cells.shape[dim] - width, cells.shape[dim], axis=dim)
        cells = jnp.concatenate(
            [
                lax.ppermute(tail, axis, [(i, (i + 1) % count) for i in range(ends)]),
                cells,
                lax.ppermute(head, axis, [((i + 1) % count, i) for i in range(ends)]),
            ],
            axis=dim,
        )
    return cells


def deriv_x(values):
    return 0.5 * (jnp.roll(values, -1, -1) - jnp.roll(values, 1, -1))


def deriv_y(values):
    return 0.5 * (values[..., 2:, :] - values[..., :-2, :])


def interior(values):
    return values[..., 1:-1, :]


def tendency(base_flow, current):
    depth_total = mean_depth + base_flow[0]
    flow_u = base_flow[1]
    flow_v = base_flow[2]
    height = current[:, 0]
    zonal = current[:, 1]
    meridional = current[:, 2]
    flux_x = depth_total * zonal + height * flow_u
    flux_y = depth_total * meridional + height * flow_v
    height_rate = -(interior(deriv_x(flux_x)) + deriv_y(flux_y))
    zonal_mid = interior(zonal)
    merid_mid = interior(meridional)
    flow_umid = interior(flow_u)
    flow_vmid = interior(flow_v)
    zonal_rate = (
        -(
            flow_umid * interior(deriv_x(zonal))
            + zonal_mid * interior(deriv_x(flow_u))
            + flow_vmid * deriv_y(zonal)
            + merid_mid * deriv_y(flow_u)
        )
        + coriolis * merid_mid
        - gravity * interior(deriv_x(height))
    )
    merid_rate = (
        -(
            flow_umid * interior(deriv_x(meridional))
            + zonal_mid * interior(deriv_x(flow_v))
            + flow_vmid * deriv_y(meridional)
            + merid_mid * deriv_y(flow_v)
        )
        - coriolis * zonal_mid
        - gravity * deriv_y(height)
    )
    return jnp.stack([height_rate, zonal_rate, merid_rate], 1)


def step_wide(base_wide, state_wide, wet_wide):
    slope_one = tendency(base_wide, state_wide)
    middle = wet_wide[1:-1] * (state_wide[:, :, 1:-1] + time_step * slope_one)
    slope_two = tendency(base_wide[:, 1:-1], middle)
    return wet_wide[2:-2] * (
        state_wide[:, :, 2:-2] + 0.5 * time_step * (slope_one[:, :, 1:-1] + slope_two)
    )


def on_device(tangents, checkpoints, owner_order, land_mask, coefficients):
    wet_mask = land_mask.astype(jnp.float32)
    current = wet_mask * tangents
    depth = 2
    flows_wide, wet_stack = (
        padded(checkpoints, (("rows", 2),), depth),
        padded(wet_mask[None, None], (("rows", 2),), depth),
    )
    wet_wide = wet_stack[0, 0]

    def fetch_flow(step_index):
        held_tile = lax.dynamic_index_in_dim(flows_wide, owner_order[step_index], 0, keepdims=False)
        return lax.all_gather(held_tile, "mode", axis=2, tiled=True)

    total_steps = owner_order.shape[0]

    def advance(step_index, current):
        widened = padded(current, (("rows", 2),), 2)
        return step_wide(fetch_flow(step_index), widened, wet_wide)

    final = lax.fori_loop(0, total_steps, advance, current)
    mixing = jnp.eye(coefficients.shape[0], dtype=jnp.float32) + jnp.triu(coefficients)
    cell_block = lax.all_to_all(final, "mode", split_axis=3, concat_axis=0, tiled=True)
    flattened = cell_block.reshape(cell_block.shape[0], -1)
    mixed = jnp.dot(
        mixing.T, flattened, precision=lax.Precision.HIGHEST, preferred_element_type=jnp.float32
    )
    return mixed.reshape(cell_block.shape)


def solution(mesh):
    placed = (
        P("mode", None, "rows", None),
        P(None, None, "rows", "mode"),
        P(),
        P("rows", None),
        P(),
    )
    return jax.shard_map(
        on_device,
        mesh=mesh,
        in_specs=placed,
        out_specs=P(None, None, "rows", "mode"),
        check_vma=False,
    )
```

profile of v0, /device:TPU:0, one launch (start us, length us, event | category | flops | bytes accessed | tf_op | source)
XLA Modules:
  0.0 402.4 jit_solution(8135360196230346554)
XLA Ops:
  1.0 5.0 %collective-permute-start.4 = (f32[8,3,2,128]{3,2,1,0:T(2,128)S(1)}, f32[8,3,2,128]{3,2,1,0:T(2,128)S(1)}, u32[]{:S(2)}, u32[]{:S(2)}) collective-permute-start(f32[8,3,2,128]{3,2,1,0:T(2,128)S(1)} %get-tuple-element.196), channel_id=1, source_target_pairs={{0,1},{1,2},{2,3},{4,5},{5,6},{6,7},{8,9},{9,10},{10,11},{12,13},{... | collective-permute-start | bytes 73736 | tf_op jit(solution)/shard_map/ppermute | solution.py:20
  6.0 1.3 collective-permute-start.5
  8.0 4.5 %collective-permute-start.2 = (f32[1,1,2,1024]{3,2,1,0:T(2,128)S(1)}, f32[1,1,2,1024]{3,2,1,0:T(2,128)S(1)}, u32[]{:S(2)}, u32[]{:S(2)}) collective-permute-start(f32[1,1,2,1024]{3,2,1,0:T(2,128)S(1)} %get-tuple-element.198), channel_id=1, source_target_pairs={{0,1},{1,2},{2,3},{4,5},{5,6},{6,7},{8,9},{9,10},{10,11},{12,13},{... | collective-permute-start | bytes 24584 | tf_op jit(solution)/shard_map/ppermute | solution.py:20
  12.6 1.3 collective-permute-start.3
  13.9 1.6 broadcast_multiply_fusion.1
  15.6 2.6 collective-permute-done.3
  18.8 316.0 %while.13 = (s32[]{:T(128)}, f32[16,3,8,1024]{3,2,1,0:T(8,128)S(1)}, f32[12,1024]{1,0:T(8,128)}, s32[8]{0:T(128)S(1)}, f32[8,3,12,128]{3,2,1,0:T(8,128)S(1)}, /*...) while((s32[]{:T(128)}, f32[16,3,8,1024]{3,2,1,0:T(8,128)S(1)}, f32[12,1024]{1,0:T(8,128)}, s32[8]{0:T(128)S(1)}, ...), condition=%wide.region_1.2_spmd, body=%wide.region_0.1_spmd.sunk | while | flops 21987332 | bytes 97589864 | solution.py:107
  19.2 1.3 collective-permute-start
  20.5 5.3 %collective-permute-start.1 = (f32[16,3,2,1024]{3,2,0,1:T(2,128)S(1)}, f32[16,3,2,1024]{3,2,0,1:T(2,128)}, u32[]{:S(2)}, u32[]{:S(2)}) collective-permute-start(f32[16,3,2,1024]{3,2,0,1:T(2,128)S(1)} %get-tuple-element.308), channel_id=1, source_target_pairs={{0,1},{1,2},{2,3},{4,5},{5,6},{6,7},{8,9},{9,10},{10,11},{12,13},{... | collective-permute-start | bytes 1179656 | tf_op jit(solution)/shard_map/while/body/eval_jaxpr/ppermute | solution.py:20
  28.5 9.6 %all-gather.2 = f32[1,3,12,1024]{3,2,1,0:T(8,128)S(1)} all-gather(f32[1,3,12,128]{3,2,1,0:T(8,128)S(1)} %constant_dynamic-slice_fusion.2), channel_id=2, replica_groups=mesh['mode'=8,'rows'=4] {'mode'}, dimensions={3}, use_global_device_ids=true | all-gather | bytes 165888 | tf_op jit(solution)/shard_map/while/body/eval_jaxpr/all_gather | solution.py:99
  43.5 1.5 pad_maximum_fusion.29
  49.6 1.6 fusion.175
  51.2 1.4 pad_maximum_fusion.30
  59.0 1.3 collective-permute-start
  60.3 5.3 %collective-permute-start.1 = (f32[16,3,2,1024]{3,2,0,1:T(2,128)S(1)}, f32[16,3,2,1024]{3,2,0,1:T(2,128)}, u32[]{:S(2)}, u32[]{:S(2)}) collective-permute-start(f32[16,3,2,1024]{3,2,0,1:T(2,128)S(1)} %get-tuple-element.308), channel_id=1, source_target_pairs={{0,1},{1,2},{2,3},{4,5},{5,6},{6,7},{8,9},{9,10},{10,11},{12,13},{... | collective-permute-start | bytes 1179656 | tf_op jit(solution)/shard_map/while/body/eval_jaxpr/ppermute | solution.py:20
  68.4 9.6 %all-gather.2 = f32[1,3,12,1024]{3,2,1,0:T(8,128)S(1)} all-gather(f32[1,3,12,128]{3,2,1,0:T(8,128)S(1)} %constant_dynamic-slice_fusion.2), channel_id=2, replica_groups=mesh['mode'=8,'rows'=4] {'mode'}, dimensions={3}, use_global_device_ids=true | all-gather | bytes 165888 | tf_op jit(solution)/shard_map/while/body/eval_jaxpr/all_gather | solution.py:99
  83.3 1.5 pad_maximum_fusion.29
  89.4 1.6 fusion.175
  91.1 1.4 pad_maximum_fusion.30
  98.9 1.3 collective-permute-start
  100.2 5.3 %collective-permute-start.1 = (f32[16,3,2,1024]{3,2,0,1:T(2,128)S(1)}, f32[16,3,2,1024]{3,2,0,1:T(2,128)}, u32[]{:S(2)}, u32[]{:S(2)}) collective-permute-start(f32[16,3,2,1024]{3,2,0,1:T(2,128)S(1)} %get-tuple-element.308), channel_id=1, source_target_pairs={{0,1},{1,2},{2,3},{4,5},{5,6},{6,7},{8,9},{9,10},{10,11},{12,13},{... | collective-permute-start | bytes 1179656 | tf_op jit(solution)/shard_map/while/body/eval_jaxpr/ppermute | solution.py:20
  108.2 8.6 %all-gather.2 = f32[1,3,12,1024]{3,2,1,0:T(8,128)S(1)} all-gather(f32[1,3,12,128]{3,2,1,0:T(8,128)S(1)} %constant_dynamic-slice_fusion.2), channel_id=2, replica_groups=mesh['mode'=8,'rows'=4] {'mode'}, dimensions={3}, use_global_device_ids=true | all-gather | bytes 165888 | tf_op jit(solution)/shard_map/while/body/eval_jaxpr/all_gather | solution.py:99
  122.2 1.5 pad_maximum_fusion.29
  128.3 1.6 fusion.175
  130.0 1.4 pad_maximum_fusion.30
  137.7 1.3 collective-permute-start
  139.0 5.3 %collective-permute-start.1 = (f32[16,3,2,1024]{3,2,0,1:T(2,128)S(1)}, f32[16,3,2,1024]{3,2,0,1:T(2,128)}, u32[]{:S(2)}, u32[]{:S(2)}) collective-permute-start(f32[16,3,2,1024]{3,2,0,1:T(2,128)S(1)} %get-tuple-element.308), channel_id=1, source_target_pairs={{0,1},{1,2},{2,3},{4,5},{5,6},{6,7},{8,9},{9,10},{10,11},{12,13},{... | collective-permute-start | bytes 1179656 | tf_op jit(solution)/shard_map/while/body/eval_jaxpr/ppermute | solution.py:20
  147.1 9.6 %all-gather.2 = f32[1,3,12,1024]{3,2,1,0:T(8,128)S(1)} all-gather(f32[1,3,12,128]{3,2,1,0:T(8,128)S(1)} %constant_dynamic-slice_fusion.2), channel_id=2, replica_groups=mesh['mode'=8,'rows'=4] {'mode'}, dimensions={3}, use_global_device_ids=true | all-gather | bytes 165888 | tf_op jit(solution)/shard_map/while/body/eval_jaxpr/all_gather | solution.py:99
  162.1 1.5 pad_maximum_fusion.29
  168.2 1.6 fusion.175
  169.8 1.4 pad_maximum_fusion.30
  177.6 1.3 collective-permute-start
  178.9 5.3 %collective-permute-start.1 = (f32[16,3,2,1024]{3,2,0,1:T(2,128)S(1)}, f32[16,3,2,1024]{3,2,0,1:T(2,128)}, u32[]{:S(2)}, u32[]{:S(2)}) collective-permute-start(f32[16,3,2,1024]{3,2,0,1:T(2,128)S(1)} %get-tuple-element.308), channel_id=1, source_target_pairs={{0,1},{1,2},{2,3},{4,5},{5,6},{6,7},{8,9},{9,10},{10,11},{12,13},{... | collective-permute-start | bytes 1179656 | tf_op jit(solution)/shard_map/while/body/eval_jaxpr/ppermute | solution.py:20
  186.9 8.6 %all-gather.2 = f32[1,3,12,1024]{3,2,1,0:T(8,128)S(1)} all-gather(f32[1,3,12,128]{3,2,1,0:T(8,128)S(1)} %constant_dynamic-slice_fusion.2), channel_id=2, replica_groups=mesh['mode'=8,'rows'=4] {'mode'}, dimensions={3}, use_global_device_ids=true | all-gather | bytes 165888 | tf_op jit(solution)/shard_map/while/body/eval_jaxpr/all_gather | solution.py:99
  200.9 1.5 pad_maximum_fusion.29
  207.1 1.6 fusion.175
  208.7 1.4 pad_maximum_fusion.30
  216.5 1.3 collective-permute-start
  217.8 5.3 %collective-permute-start.1 = (f32[16,3,2,1024]{3,2,0,1:T(2,128)S(1)}, f32[16,3,2,1024]{3,2,0,1:T(2,128)}, u32[]{:S(2)}, u32[]{:S(2)}) collective-permute-start(f32[16,3,2,1024]{3,2,0,1:T(2,128)S(1)} %get-tuple-element.308), channel_id=1, source_target_pairs={{0,1},{1,2},{2,3},{4,5},{5,6},{6,7},{8,9},{9,10},{10,11},{12,13},{... | collective-permute-start | bytes 1179656 | tf_op jit(solution)/shard_map/while/body/eval_jaxpr/ppermute | solution.py:20
  225.8 9.6 %all-gather.2 = f32[1,3,12,1024]{3,2,1,0:T(8,128)S(1)} all-gather(f32[1,3,12,128]{3,2,1,0:T(8,128)S(1)} %constant_dynamic-slice_fusion.2), channel_id=2, replica_groups=mesh['mode'=8,'rows'=4] {'mode'}, dimensions={3}, use_global_device_ids=true | all-gather | bytes 165888 | tf_op jit(solution)/shard_map/while/body/eval_jaxpr/all_gather | solution.py:99
  240.8 1.5 pad_maximum_fusion.29
  246.9 1.6 fusion.175
  248.5 1.4 pad_maximum_fusion.30
  256.3 1.3 collective-permute-start
  257.6 5.3 %collective-permute-start.1 = (f32[16,3,2,1024]{3,2,0,1:T(2,128)S(1)}, f32[16,3,2,1024]{3,2,0,1:T(2,128)}, u32[]{:S(2)}, u32[]{:S(2)}) collective-permute-start(f32[16,3,2,1024]{3,2,0,1:T(2,128)S(1)} %get-tuple-element.308), channel_id=1, source_target_pairs={{0,1},{1,2},{2,3},{4,5},{5,6},{6,7},{8,9},{9,10},{10,11},{12,13},{... | collective-permute-start | bytes 1179656 | tf_op jit(solution)/shard_map/while/body/eval_jaxpr/ppermute | solution.py:20
  265.6 8.6 %all-gather.2 = f32[1,3,12,1024]{3,2,1,0:T(8,128)S(1)} all-gather(f32[1,3,12,128]{3,2,1,0:T(8,128)S(1)} %constant_dynamic-slice_fusion.2), channel_id=2, replica_groups=mesh['mode'=8,'rows'=4] {'mode'}, dimensions={3}, use_global_device_ids=true | all-gather | bytes 165888 | tf_op jit(solution)/shard_map/while/body/eval_jaxpr/all_gather | solution.py:99
  279.7 1.5 pad_maximum_fusion.29
  285.8 1.6 fusion.175
  287.4 1.4 pad_maximum_fusion.30
  295.2 1.3 collective-permute-start
  296.5 5.3 %collective-permute-start.1 = (f32[16,3,2,1024]{3,2,0,1:T(2,128)S(1)}, f32[16,3,2,1024]{3,2,0,1:T(2,128)}, u32[]{:S(2)}, u32[]{:S(2)}) collective-permute-start(f32[16,3,2,1024]{3,2,0,1:T(2,128)S(1)} %get-tuple-element.308), channel_id=1, source_target_pairs={{0,1},{1,2},{2,3},{4,5},{5,6},{6,7},{8,9},{9,10},{10,11},{12,13},{... | collective-permute-start | bytes 1179656 | tf_op jit(solution)/shard_map/while/body/eval_jaxpr/ppermute | solution.py:20
  304.5 9.6 %all-gather.2 = f32[1,3,12,1024]{3,2,1,0:T(8,128)S(1)} all-gather(f32[1,3,12,128]{3,2,1,0:T(8,128)S(1)} %constant_dynamic-slice_fusion.2), channel_id=2, replica_groups=mesh['mode'=8,'rows'=4] {'mode'}, dimensions={3}, use_global_device_ids=true | all-gather | bytes 165888 | tf_op jit(solution)/shard_map/while/body/eval_jaxpr/all_gather | solution.py:99
  319.5 1.5 pad_maximum_fusion.29
  325.6 1.6 fusion.175
  327.2 1.4 pad_maximum_fusion.30
  334.9 7.4 %copy.42 = f32[16,3,8,1024]{0,2,1,3:T(8,128)} copy(f32[16,3,8,1024]{3,2,1,0:T(8,128)S(1)} %get-tuple-element.418) | data formatting | bytes 3145728 | tf_op jit(solution)/shard_map/while | solution.py:107
  342.3 9.8 %reshape.42 = f32[8,1,49152]{2,1,0:T(1,128)} reshape(f32[1024,3,8,16]{3,2,1,0:T(8,128)} %bitcast.127) | data formatting | bytes 3145728
  352.1 3.6 all-to-all-start
  355.7 20.9 %all-to-all-done = f32[8,1,49152]{2,1,0:T(1,128)S(1)} async-done(((f32[8,1,49152]{2,1,0:T(1,128)}), f32[8,1,49152]{2,1,0:T(1,128)S(1)}, u32[]{:S(2)}, u32[]{:S(2)}) %all-to-all-start) | async-done | bytes 1572896 | tf_op jit(solution)/shard_map/all_to_all | solution.py:109
  377.1 4.4 %reduce = f32[8,49152]{1,0:T(8,128)S(1)} reduce(f32[8,1,49152]{2,1,0:T(1,128)S(1)} %all-to-all-done, f32[]{:T(128)} %broadcast.142), dimensions={1}, to_apply=%all_to_all.11.reduce_sub_computation | reduce | bytes 3145732 | tf_op jit(solution)/shard_map/all_to_all | solution.py:109
  381.5 8.7 %reshape.43 = f32[1024,3,8,16]{3,2,1,0:T(8,128)} reshape(f32[8,49152]{1,0:T(8,128)S(1)} %reduce) | data formatting | bytes 3145728
  390.2 7.5 %copy.43 = f32[16,3,8,8,128]{4,2,1,0,3:T(8,128)S(1)} copy(f32[16,3,8,8,128]{0,2,1,4,3:T(8,128)} %bitcast.128) | data formatting | bytes 3145728 | tf_op jit(solution)/shard_map/all_to_all | solution.py:109
  398.8 1.5 fusion.85
  400.3 2.1 copy.46
  (506 shorter events, 138.3 us)
Async XLA Ops:
  1.0 17.8 %collective-permute-start.4 = (f32[8,3,2,128]{3,2,1,0:T(2,128)S(1)}, f32[8,3,2,128]{3,2,1,0:T(2,128)S(1)}, u32[]{:S(2)}, u32[]{:S(2)}) collective-permute-start(f32[8,3,2,128]{3,2,1,0:T(2,128)S(1)} %get-tuple-element.196), channel_id=1, source_target_pairs={{0,1},{1,2},{2,3},{4,5},{5,6},{6,7},{8,9},{9,10},{10,11},{12,13},{... | collective-permute-start | bytes 73736 | tf_op jit(solution)/shard_map/ppermute | solution.py:20
  6.0 12.8 %collective-permute-start.5 = (f32[8,3,2,128]{3,2,1,0:T(2,128)S(1)}, f32[8,3,2,128]{3,2,1,0:T(2,128)S(1)}, u32[]{:S(2)}, u32[]{:S(2)}) collective-permute-start(f32[8,3,2,128]{3,2,1,0:T(2,128)S(1)} %get-tuple-element.197), channel_id=1, source_target_pairs={{1,0},{2,1},{3,2},{5,4},{6,5},{7,6},{9,8},{10,9},{11,10},{13,12},{... | collective-permute-start | bytes 73736 | tf_op jit(solution)/shard_map/ppermute | solution.py:22
  8.0 7.5 %collective-permute-start.2 = (f32[1,1,2,1024]{3,2,1,0:T(2,128)S(1)}, f32[1,1,2,1024]{3,2,1,0:T(2,128)S(1)}, u32[]{:S(2)}, u32[]{:S(2)}) collective-permute-start(f32[1,1,2,1024]{3,2,1,0:T(2,128)S(1)} %get-tuple-element.198), channel_id=1, source_target_pairs={{0,1},{1,2},{2,3},{4,5},{5,6},{6,7},{8,9},{9,10},{10,11},{12,13},{... | collective-permute-start | bytes 24584 | tf_op jit(solution)/shard_map/ppermute | solution.py:20
  12.6 5.5 %collective-permute-start.3 = (f32[1,1,2,1024]{3,2,1,0:T(2,128)S(1)}, f32[1,1,2,1024]{3,2,1,0:T(2,128)S(1)}, u32[]{:S(2)}, u32[]{:S(2)}) collective-permute-start(f32[1,1,2,1024]{3,2,1,0:T(2,128)S(1)} %get-tuple-element.199), channel_id=1, source_target_pairs={{1,0},{2,1},{3,2},{5,4},{6,5},{7,6},{9,8},{10,9},{11,10},{13,12},{... | collective-permute-start | bytes 24584 | tf_op jit(solution)/shard_map/ppermute | solution.py:22
  13.9 4.9 %copy-start.8 = (f32[8,3,8,128]{3,2,1,0:T(8,128)S(1)}, f32[8,3,8,128]{3,2,1,0:T(8,128)}, u32[]{:S(2)}) copy-start(f32[8,3,8,128]{3,2,1,0:T(8,128)} %param.8) | copy-start | bytes 294916
  13.9 4.9 %copy-start.10 = (s32[8]{0:T(128)S(1)}, s32[8]{0:T(128)}, u32[]{:S(2)}) copy-start(s32[8]{0:T(128)} %param.9) | copy-start | bytes 100
  18.9 20.7 %copy-start.6 = (f32[8,3,12,128]{3,2,1,0:T(8,128)}, f32[8,3,12,128]{3,2,1,0:T(8,128)S(1)}, u32[]{:S(2)}) copy-start(f32[8,3,12,128]{3,2,1,0:T(8,128)S(1)} %get-tuple-element.401) | copy-start | bytes 442372 | tf_op jit(solution)/shard_map/while
  19.2 24.3 %collective-permute-start = (f32[16,3,2,1024]{3,2,0,1:T(2,128)S(1)}, f32[16,3,2,1024]{3,2,0,1:T(2,128)S(1)}, u32[]{:S(2)}, u32[]{:S(2)}) collective-permute-start(f32[16,3,2,1024]{3,2,0,1:T(2,128)S(1)} %get-tuple-element.307), channel_id=1, source_target_pairs={{1,0},{2,1},{3,2},{5,4},{6,5},{7,6},{9,8},{10,9},{11,10},{13,12},{... | collective-permute-start | bytes 1179656 | tf_op jit(solution)/shard_map/while/body/eval_jaxpr/ppermute | solution.py:22
  20.5 23.0 %collective-permute-start.1 = (f32[16,3,2,1024]{3,2,0,1:T(2,128)S(1)}, f32[16,3,2,1024]{3,2,0,1:T(2,128)}, u32[]{:S(2)}, u32[]{:S(2)}) collective-permute-start(f32[16,3,2,1024]{3,2,0,1:T(2,128)S(1)} %get-tuple-element.308), channel_id=1, source_target_pairs={{0,1},{1,2},{2,3},{4,5},{5,6},{6,7},{8,9},{9,10},{10,11},{12,13},{... | collective-permute-start | bytes 1179656 | tf_op jit(solution)/shard_map/while/body/eval_jaxpr/ppermute | solution.py:20
  38.1 3.8 copy-start.2
  43.5 1.6 copy-start.1
  57.7 1.0 copy-start.7
  57.7 1.0 copy-start.11
  58.7 20.6 %copy-start.6 = (f32[8,3,12,128]{3,2,1,0:T(8,128)}, f32[8,3,12,128]{3,2,1,0:T(8,128)S(1)}, u32[]{:S(2)}) copy-start(f32[8,3,12,128]{3,2,1,0:T(8,128)S(1)} %get-tuple-element.401) | copy-start | bytes 442372 | tf_op jit(solution)/shard_map/while
  59.0 24.3 %collective-permute-start = (f32[16,3,2,1024]{3,2,0,1:T(2,128)S(1)}, f32[16,3,2,1024]{3,2,0,1:T(2,128)S(1)}, u32[]{:S(2)}, u32[]{:S(2)}) collective-permute-start(f32[16,3,2,1024]{3,2,0,1:T(2,128)S(1)} %get-tuple-element.307), channel_id=1, source_target_pairs={{1,0},{2,1},{3,2},{5,4},{6,5},{7,6},{9,8},{10,9},{11,10},{13,12},{... | collective-permute-start | bytes 1179656 | tf_op jit(solution)/shard_map/while/body/eval_jaxpr/ppermute | solution.py:22
  60.3 23.0 %collective-permute-start.1 = (f32[16,3,2,1024]{3,2,0,1:T(2,128)S(1)}, f32[16,3,2,1024]{3,2,0,1:T(2,128)}, u32[]{:S(2)}, u32[]{:S(2)}) collective-permute-start(f32[16,3,2,1024]{3,2,0,1:T(2,128)S(1)} %get-tuple-element.308), channel_id=1, source_target_pairs={{0,1},{1,2},{2,3},{4,5},{5,6},{6,7},{8,9},{9,10},{10,11},{12,13},{... | collective-permute-start | bytes 1179656 | tf_op jit(solution)/shard_map/while/body/eval_jaxpr/ppermute | solution.py:20
  77.9 3.8 copy-start.2
  83.3 1.6 copy-start.1
  97.5 1.0 copy-start.7
  97.5 1.0 copy-start.11
  98.6 19.7 %copy-start.6 = (f32[8,3,12,128]{3,2,1,0:T(8,128)}, f32[8,3,12,128]{3,2,1,0:T(8,128)S(1)}, u32[]{:S(2)}) copy-start(f32[8,3,12,128]{3,2,1,0:T(8,128)S(1)} %get-tuple-element.401) | copy-start | bytes 442372 | tf_op jit(solution)/shard_map/while
  98.9 23.4 %collective-permute-start = (f32[16,3,2,1024]{3,2,0,1:T(2,128)S(1)}, f32[16,3,2,1024]{3,2,0,1:T(2,128)S(1)}, u32[]{:S(2)}, u32[]{:S(2)}) collective-permute-start(f32[16,3,2,1024]{3,2,0,1:T(2,128)S(1)} %get-tuple-element.307), channel_id=1, source_target_pairs={{1,0},{2,1},{3,2},{5,4},{6,5},{7,6},{9,8},{10,9},{11,10},{13,12},{... | collective-permute-start | bytes 1179656 | tf_op jit(solution)/shard_map/while/body/eval_jaxpr/ppermute | solution.py:22
  100.2 22.1 %collective-permute-start.1 = (f32[16,3,2,1024]{3,2,0,1:T(2,128)S(1)}, f32[16,3,2,1024]{3,2,0,1:T(2,128)}, u32[]{:S(2)}, u32[]{:S(2)}) collective-permute-start(f32[16,3,2,1024]{3,2,0,1:T(2,128)S(1)} %get-tuple-element.308), channel_id=1, source_target_pairs={{0,1},{1,2},{2,3},{4,5},{5,6},{6,7},{8,9},{9,10},{10,11},{12,13},{... | collective-permute-start | bytes 1179656 | tf_op jit(solution)/shard_map/while/body/eval_jaxpr/ppermute | solution.py:20
  116.8 3.8 copy-start.2
  122.2 1.6 copy-start.1
  136.4 1.0 copy-start.7
  136.4 1.0 copy-start.11
  137.4 20.6 %copy-start.6 = (f32[8,3,12,128]{3,2,1,0:T(8,128)}, f32[8,3,12,128]{3,2,1,0:T(8,128)S(1)}, u32[]{:S(2)}) copy-start(f32[8,3,12,128]{3,2,1,0:T(8,128)S(1)} %get-tuple-element.401) | copy-start | bytes 442372 | tf_op jit(solution)/shard_map/while
  137.7 24.3 %collective-permute-start = (f32[16,3,2,1024]{3,2,0,1:T(2,128)S(1)}, f32[16,3,2,1024]{3,2,0,1:T(2,128)S(1)}, u32[]{:S(2)}, u32[]{:S(2)}) collective-permute-start(f32[16,3,2,1024]{3,2,0,1:T(2,128)S(1)} %get-tuple-element.307), channel_id=1, source_target_pairs={{1,0},{2,1},{3,2},{5,4},{6,5},{7,6},{9,8},{10,9},{11,10},{13,12},{... | collective-permute-start | bytes 1179656 | tf_op jit(solution)/shard_map/while/body/eval_jaxpr/ppermute | solution.py:22
  139.0 23.0 %collective-permute-start.1 = (f32[16,3,2,1024]{3,2,0,1:T(2,128)S(1)}, f32[16,3,2,1024]{3,2,0,1:T(2,128)}, u32[]{:S(2)}, u32[]{:S(2)}) collective-permute-start(f32[16,3,2,1024]{3,2,0,1:T(2,128)S(1)} %get-tuple-element.308), channel_id=1, source_target_pairs={{0,1},{1,2},{2,3},{4,5},{5,6},{6,7},{8,9},{9,10},{10,11},{12,13},{... | collective-permute-start | bytes 1179656 | tf_op jit(solution)/shard_map/while/body/eval_jaxpr/ppermute | solution.py:20
  156.6 3.8 copy-start.2
  162.0 1.6 copy-start.1
  176.2 1.0 copy-start.7
  176.2 1.0 copy-start.11
  177.3 19.7 %copy-start.6 = (f32[8,3,12,128]{3,2,1,0:T(8,128)}, f32[8,3,12,128]{3,2,1,0:T(8,128)S(1)}, u32[]{:S(2)}) copy-start(f32[8,3,12,128]{3,2,1,0:T(8,128)S(1)} %get-tuple-element.401) | copy-start | bytes 442372 | tf_op jit(solution)/shard_map/while
  177.6 23.4 %collective-permute-start = (f32[16,3,2,1024]{3,2,0,1:T(2,128)S(1)}, f32[16,3,2,1024]{3,2,0,1:T(2,128)S(1)}, u32[]{:S(2)}, u32[]{:S(2)}) collective-permute-start(f32[16,3,2,1024]{3,2,0,1:T(2,128)S(1)} %get-tuple-element.307), channel_id=1, source_target_pairs={{1,0},{2,1},{3,2},{5,4},{6,5},{7,6},{9,8},{10,9},{11,10},{13,12},{... | collective-permute-start | bytes 1179656 | tf_op jit(solution)/shard_map/while/body/eval_jaxpr/ppermute | solution.py:22
  178.9 22.1 %collective-permute-start.1 = (f32[16,3,2,1024]{3,2,0,1:T(2,128)S(1)}, f32[16,3,2,1024]{3,2,0,1:T(2,128)}, u32[]{:S(2)}, u32[]{:S(2)}) collective-permute-start(f32[16,3,2,1024]{3,2,0,1:T(2,128)S(1)} %get-tuple-element.308), channel_id=1, source_target_pairs={{0,1},{1,2},{2,3},{4,5},{5,6},{6,7},{8,9},{9,10},{10,11},{12,13},{... | collective-permute-start | bytes 1179656 | tf_op jit(solution)/shard_map/while/body/eval_jaxpr/ppermute | solution.py:20
  195.5 3.8 copy-start.2
  200.9 1.6 copy-start.1
  215.1 1.0 copy-start.7
  215.1 1.0 copy-start.11
  216.2 20.6 %copy-start.6 = (f32[8,3,12,128]{3,2,1,0:T(8,128)}, f32[8,3,12,128]{3,2,1,0:T(8,128)S(1)}, u32[]{:S(2)}) copy-start(f32[8,3,12,128]{3,2,1,0:T(8,128)S(1)} %get-tuple-element.401) | copy-start | bytes 442372 | tf_op jit(solution)/shard_map/while
  216.5 24.3 %collective-permute-start = (f32[16,3,2,1024]{3,2,0,1:T(2,128)S(1)}, f32[16,3,2,1024]{3,2,0,1:T(2,128)S(1)}, u32[]{:S(2)}, u32[]{:S(2)}) collective-permute-start(f32[16,3,2,1024]{3,2,0,1:T(2,128)S(1)} %get-tuple-element.307), channel_id=1, source_target_pairs={{1,0},{2,1},{3,2},{5,4},{6,5},{7,6},{9,8},{10,9},{11,10},{13,12},{... | collective-permute-start | bytes 1179656 | tf_op jit(solution)/shard_map/while/body/eval_jaxpr/ppermute | solution.py:22
  217.8 23.0 %collective-permute-start.1 = (f32[16,3,2,1024]{3,2,0,1:T(2,128)S(1)}, f32[16,3,2,1024]{3,2,0,1:T(2,128)}, u32[]{:S(2)}, u32[]{:S(2)}) collective-permute-start(f32[16,3,2,1024]{3,2,0,1:T(2,128)S(1)} %get-tuple-element.308), channel_id=1, source_target_pairs={{0,1},{1,2},{2,3},{4,5},{5,6},{6,7},{8,9},{9,10},{10,11},{12,13},{... | collective-permute-start | bytes 1179656 | tf_op jit(solution)/shard_map/while/body/eval_jaxpr/ppermute | solution.py:20
  235.4 3.8 copy-start.2
  240.8 1.6 copy-start.1
  255.0 1.0 copy-start.7
  255.0 1.0 copy-start.11
  256.0 19.7 %copy-start.6 = (f32[8,3,12,128]{3,2,1,0:T(8,128)}, f32[8,3,12,128]{3,2,1,0:T(8,128)S(1)}, u32[]{:S(2)}) copy-start(f32[8,3,12,128]{3,2,1,0:T(8,128)S(1)} %get-tuple-element.401) | copy-start | bytes 442372 | tf_op jit(solution)/shard_map/while
  256.3 23.4 %collective-permute-start = (f32[16,3,2,1024]{3,2,0,1:T(2,128)S(1)}, f32[16,3,2,1024]{3,2,0,1:T(2,128)S(1)}, u32[]{:S(2)}, u32[]{:S(2)}) collective-permute-start(f32[16,3,2,1024]{3,2,0,1:T(2,128)S(1)} %get-tuple-element.307), channel_id=1, source_target_pairs={{1,0},{2,1},{3,2},{5,4},{6,5},{7,6},{9,8},{10,9},{11,10},{13,12},{... | collective-permute-start | bytes 1179656 | tf_op jit(solution)/shard_map/while/body/eval_jaxpr/ppermute | solution.py:22
  257.6 22.1 %collective-permute-start.1 = (f32[16,3,2,1024]{3,2,0,1:T(2,128)S(1)}, f32[16,3,2,1024]{3,2,0,1:T(2,128)}, u32[]{:S(2)}, u32[]{:S(2)}) collective-permute-start(f32[16,3,2,1024]{3,2,0,1:T(2,128)S(1)} %get-tuple-element.308), channel_id=1, source_target_pairs={{0,1},{1,2},{2,3},{4,5},{5,6},{6,7},{8,9},{9,10},{10,11},{12,13},{... | collective-permute-start | bytes 1179656 | tf_op jit(solution)/shard_map/while/body/eval_jaxpr/ppermute | solution.py:20
  274.2 3.8 copy-start.2
  279.6 1.6 copy-start.1
  293.8 1.0 copy-start.7
  293.9 1.0 copy-start.11
  294.9 20.6 %copy-start.6 = (f32[8,3,12,128]{3,2,1,0:T(8,128)}, f32[8,3,12,128]{3,2,1,0:T(8,128)S(1)}, u32[]{:S(2)}) copy-start(f32[8,3,12,128]{3,2,1,0:T(8,128)S(1)} %get-tuple-element.401) | copy-start | bytes 442372 | tf_op jit(solution)/shard_map/while
  295.2 24.3 %collective-permute-start = (f32[16,3,2,1024]{3,2,0,1:T(2,128)S(1)}, f32[16,3,2,1024]{3,2,0,1:T(2,128)S(1)}, u32[]{:S(2)}, u32[]{:S(2)}) collective-permute-start(f32[16,3,2,1024]{3,2,0,1:T(2,128)S(1)} %get-tuple-element.307), channel_id=1, source_target_pairs={{1,0},{2,1},{3,2},{5,4},{6,5},{7,6},{9,8},{10,9},{11,10},{13,12},{... | collective-permute-start | bytes 1179656 | tf_op jit(solution)/shard_map/while/body/eval_jaxpr/ppermute | solution.py:22
  296.5 23.0 %collective-permute-start.1 = (f32[16,3,2,1024]{3,2,0,1:T(2,128)S(1)}, f32[16,3,2,1024]{3,2,0,1:T(2,128)}, u32[]{:S(2)}, u32[]{:S(2)}) collective-permute-start(f32[16,3,2,1024]{3,2,0,1:T(2,128)S(1)} %get-tuple-element.308), channel_id=1, source_target_pairs={{0,1},{1,2},{2,3},{4,5},{5,6},{6,7},{8,9},{9,10},{10,11},{12,13},{... | collective-permute-start | bytes 1179656 | tf_op jit(solution)/shard_map/while/body/eval_jaxpr/ppermute | solution.py:20
  314.1 3.8 copy-start.2
  319.5 1.6 copy-start.1
  333.7 1.0 copy-start.7
  333.7 1.0 copy-start.11
  352.1 24.5 %all-to-all-start = ((f32[8,1,49152]{2,1,0:T(1,128)}), f32[8,1,49152]{2,1,0:T(1,128)S(1)}, u32[]{:S(2)}, u32[]{:S(2)}) async-start(f32[8,1,49152]{2,1,0:T(1,128)} %reshape.42), calls=%async_computation | async-start | bytes 3145728 | tf_op jit(solution)/shard_map/all_to_all | solution.py:109
  397.9 0.8 copy-start.9
  (32 other events, 25.4 us)
where the time goes:
time: 406 us; the launch traced here: 402 us
  other arithmetic  119 us (29%)
  local copies, waits for them, and re-layouts  97 us (24%)
  blocking collectives  73.6 us (18%)
  starting transfers between devices  68.4 us (17%)
  waiting for transfers between devices  23.5 us (6%)
  loops' own time  19.3 us (5%)
    all_gather x8, blocking collectives, fetch_flow(): return lax.all_gather(held_tile, 'mode', axis=2, tiled=True)  73.6 us
    another operation x56, other arithmetic, tendency(): return jnp.stack([height_rate, zonal_rate, merid_rate], 1)  53.8 us
    ppermute x10, starting transfers between devices, padded(): lax.ppermute(tail, axis, [(i, (i + 1) % count) for i in range(ends)])  51.9 us
    slice x144, local copies, waits for them, and re-layouts, deriv_x(): return 0.5 * (jnp.roll(values, -1, -1) - jnp.roll(values, 1, -1))  37.2 us
    mul x32, other arithmetic, deriv_x(): return 0.5 * (jnp.roll(values, -1, -1) - jnp.roll(values, 1, -1))  24.6 us
    all_to_all x1, waiting for transfers between devices, on_device(): lax.all_to_all(final, 'mode', split_axis=3, concat_axis=0, tiled=True)  20.9 us
    another operation x1, loops' own time, on_device(): final = lax.fori_loop(0, total_steps, advance, current)  19.3 us
    unnamed x8, local copies, waits for them, and re-layouts  18.9 us
  transfers between devices with their start and end apart: 21, of which 2 were waited for; matrix products, arithmetic and copies ran while one was open for 13% of the time, Pallas kernels for 0%

commit v1 on v0

--- a/solution.py
+++ b/solution.py
@@ -106,7 +106,10 @@
 
     final = lax.fori_loop(0, total_steps, advance, current)
     mixing = jnp.eye(coefficients.shape[0], dtype=jnp.float32) + jnp.triu(coefficients)
-    cell_block = lax.all_to_all(final, "mode", split_axis=3, concat_axis=0, tiled=True)
+    cell_block = jnp.concatenate(
+        lax.all_to_all(jnp.stack(jnp.split(final, lax.axis_size("mode"), axis=3)), "mode", 0, 0),
+        axis=0,
+    )
     flattened = cell_block.reshape(cell_block.shape[0], -1)
     mixed = jnp.dot(
         mixing.T, flattened, precision=lax.Precision.HIGHEST, preferred_element_type=jnp.float32

time: 406 us -> 373 us (0.919)
  local copies, waits for them, and re-layouts: 97 us -> 68.9 us
  other arithmetic: 119 us -> 114 us
    unnamed x8 -> x13, local copies, waits for them, and re-layouts: 18.9 us -> 5.3 us
    all_to_all x2 -> x0, local copies, waits for them, and re-layouts: 7.99 us -> none  [on_device(): lax.all_to_all(final, 'mode', split_axis=3, concat_axis=0, tiled=True)]
    while x145 -> x144, local copies, waits for them, and re-layouts: 12.7 us -> 5.34 us  [the longest x1 7.37 us: on_device(): final = lax.fori_loop(0, total_steps, advance, current)]
    all_to_all x1 -> x0, other arithmetic: 4.38 us -> none  [on_device(): lax.all_to_all(final, 'mode', split_axis=3, concat_axis=0, tiled=True)]
  transfers between devices with their start and end apart: 21 -> 21, of which waited for: 2 -> 2; matrix products, arithmetic and copies ran while one was open for 13% -> 14% of each run, Pallas kernels for 0% -> 0%
where the time goes in v1:
time: 373 us; the launch traced here: 370 us
  other arithmetic  114 us (31%)
  blocking collectives  73.6 us (20%)
  local copies, waits for them, and re-layouts  68.9 us (18%)
  starting transfers between devices  68.3 us (18%)
  waiting for transfers between devices  23.5 us (6%)
  loops' own time  19.3 us (5%)
    all_gather x8, blocking collectives, fetch_flow(): return lax.all_gather(held_tile, 'mode', axis=2, tiled=True)  73.6 us
    another operation x56, other arithmetic, tendency(): return jnp.stack([height_rate, zonal_rate, merid_rate], 1)  53.8 us
    ppermute x10, starting transfers between devices, padded(): lax.ppermute(tail, axis, [(i, (i + 1) % count) for i in range(ends)])  51.8 us
    slice x144, local copies, waits for them, and re-layouts, deriv_x(): return 0.5 * (jnp.roll(values, -1, -1) - jnp.roll(values, 1, -1))  37.3 us
    mul x32, other arithmetic, deriv_x(): return 0.5 * (jnp.roll(values, -1, -1) - jnp.roll(values, 1, -1))  24.6 us
    all_to_all x1, waiting for transfers between devices, on_device(): lax.all_to_all(jnp.stack(jnp.split(final, lax.axis_size('mode'), axis=3))...  20.9 us
    another operation x1, loops' own time, on_device(): final = lax.fori_loop(0, total_steps, advance, current)  19.3 us
    ppermute x10, starting transfers between devices, padded(): lax.ppermute(head, axis, [((i + 1) % count, i) for i in range(ends)])  12.9 us
  transfers between devices with their start and end apart: 21, of which 2 were waited for; matrix products, arithmetic and copies ran while one was open for 14% of the time, Pallas kernels for 0%

profile of v1, /device:TPU:0, one launch (start us, length us, event | category | flops | bytes accessed | tf_op | source)
XLA Modules:
  0.0 369.8 jit_solution(5539356471445465971)
XLA Ops:
  1.0 5.0 %collective-permute-start.4 = (f32[8,3,2,128]{3,2,1,0:T(2,128)S(1)}, f32[8,3,2,128]{3,2,1,0:T(2,128)S(1)}, u32[]{:S(2)}, u32[]{:S(2)}) collective-permute-start(f32[8,3,2,128]{3,2,1,0:T(2,128)S(1)} %get-tuple-element.196), channel_id=1, source_target_pairs={{0,1},{1,2},{2,3},{4,5},{5,6},{6,7},{8,9},{9,10},{10,11},{12,13},{... | collective-permute-start | bytes 73736 | tf_op jit(solution)/shard_map/ppermute | solution.py:20
  6.0 1.3 collective-permute-start.5
  8.0 4.5 %collective-permute-start.2 = (f32[1,1,2,1024]{3,2,1,0:T(2,128)S(1)}, f32[1,1,2,1024]{3,2,1,0:T(2,128)S(1)}, u32[]{:S(2)}, u32[]{:S(2)}) collective-permute-start(f32[1,1,2,1024]{3,2,1,0:T(2,128)S(1)} %get-tuple-element.198), channel_id=1, source_target_pairs={{0,1},{1,2},{2,3},{4,5},{5,6},{6,7},{8,9},{9,10},{10,11},{12,13},{... | collective-permute-start | bytes 24584 | tf_op jit(solution)/shard_map/ppermute | solution.py:20
  12.6 1.3 collective-permute-start.3
  13.9 1.6 broadcast_multiply_fusion.1
  15.6 2.6 collective-permute-done.3
  18.8 316.1 %while.13 = (s32[]{:T(128)}, f32[16,3,8,1024]{3,2,1,0:T(8,128)S(1)}, f32[12,1024]{1,0:T(8,128)}, s32[8]{0:T(128)S(1)}, f32[8,3,12,128]{3,2,1,0:T(8,128)S(1)}, /*...) while((s32[]{:T(128)}, f32[16,3,8,1024]{3,2,1,0:T(8,128)S(1)}, f32[12,1024]{1,0:T(8,128)}, s32[8]{0:T(128)S(1)}, ...), condition=%wide.region_1.2_spmd, body=%wide.region_0.1_spmd.sunk | while | flops 21987332 | bytes 97589864 | solution.py:107
  19.2 1.3 collective-permute-start
  20.5 5.3 %collective-permute-start.1 = (f32[16,3,2,1024]{3,2,0,1:T(2,128)S(1)}, f32[16,3,2,1024]{3,2,0,1:T(2,128)}, u32[]{:S(2)}, u32[]{:S(2)}) collective-permute-start(f32[16,3,2,1024]{3,2,0,1:T(2,128)S(1)} %get-tuple-element.308), channel_id=1, source_target_pairs={{0,1},{1,2},{2,3},{4,5},{5,6},{6,7},{8,9},{9,10},{10,11},{12,13},{... | collective-permute-start | bytes 1179656 | tf_op jit(solution)/shard_map/while/body/eval_jaxpr/ppermute | solution.py:20
  28.5 9.6 %all-gather.2 = f32[1,3,12,1024]{3,2,1,0:T(8,128)S(1)} all-gather(f32[1,3,12,128]{3,2,1,0:T(8,128)S(1)} %constant_dynamic-slice_fusion.2), channel_id=2, replica_groups=mesh['mode'=8,'rows'=4] {'mode'}, dimensions={3}, use_global_device_ids=true | all-gather | bytes 165888 | tf_op jit(solution)/shard_map/while/body/eval_jaxpr/all_gather | solution.py:99
  43.5 1.5 pad_maximum_fusion.29
  48.4 1.2 fusion.171
  49.6 1.6 fusion.175
  51.3 1.4 pad_maximum_fusion.30
  59.0 1.3 collective-permute-start
  60.3 5.3 %collective-permute-start.1 = (f32[16,3,2,1024]{3,2,0,1:T(2,128)S(1)}, f32[16,3,2,1024]{3,2,0,1:T(2,128)}, u32[]{:S(2)}, u32[]{:S(2)}) collective-permute-start(f32[16,3,2,1024]{3,2,0,1:T(2,128)S(1)} %get-tuple-element.308), channel_id=1, source_target_pairs={{0,1},{1,2},{2,3},{4,5},{5,6},{6,7},{8,9},{9,10},{10,11},{12,13},{... | collective-permute-start | bytes 1179656 | tf_op jit(solution)/shard_map/while/body/eval_jaxpr/ppermute | solution.py:20
  68.4 9.6 %all-gather.2 = f32[1,3,12,1024]{3,2,1,0:T(8,128)S(1)} all-gather(f32[1,3,12,128]{3,2,1,0:T(8,128)S(1)} %constant_dynamic-slice_fusion.2), channel_id=2, replica_groups=mesh['mode'=8,'rows'=4] {'mode'}, dimensions={3}, use_global_device_ids=true | all-gather | bytes 165888 | tf_op jit(solution)/shard_map/while/body/eval_jaxpr/all_gather | solution.py:99
  83.4 1.5 pad_maximum_fusion.29
  88.2 1.2 fusion.171
  89.5 1.6 fusion.175
  91.1 1.4 pad_maximum_fusion.30
  98.9 1.3 collective-permute-start
  100.2 5.3 %collective-permute-start.1 = (f32[16,3,2,1024]{3,2,0,1:T(2,128)S(1)}, f32[16,3,2,1024]{3,2,0,1:T(2,128)}, u32[]{:S(2)}, u32[]{:S(2)}) collective-permute-start(f32[16,3,2,1024]{3,2,0,1:T(2,128)S(1)} %get-tuple-element.308), channel_id=1, source_target_pairs={{0,1},{1,2},{2,3},{4,5},{5,6},{6,7},{8,9},{9,10},{10,11},{12,13},{... | collective-permute-start | bytes 1179656 | tf_op jit(solution)/shard_map/while/body/eval_jaxpr/ppermute | solution.py:20
  108.2 8.6 %all-gather.2 = f32[1,3,12,1024]{3,2,1,0:T(8,128)S(1)} all-gather(f32[1,3,12,128]{3,2,1,0:T(8,128)S(1)} %constant_dynamic-slice_fusion.2), channel_id=2, replica_groups=mesh['mode'=8,'rows'=4] {'mode'}, dimensions={3}, use_global_device_ids=true | all-gather | bytes 165888 | tf_op jit(solution)/shard_map/while/body/eval_jaxpr/all_gather | solution.py:99
  122.3 1.5 pad_maximum_fusion.29
  127.1 1.2 fusion.171
  128.4 1.6 fusion.175
  130.0 1.4 pad_maximum_fusion.30
  137.8 1.3 collective-permute-start
  139.1 5.3 %collective-permute-start.1 = (f32[16,3,2,1024]{3,2,0,1:T(2,128)S(1)}, f32[16,3,2,1024]{3,2,0,1:T(2,128)}, u32[]{:S(2)}, u32[]{:S(2)}) collective-permute-start(f32[16,3,2,1024]{3,2,0,1:T(2,128)S(1)} %get-tuple-element.308), channel_id=1, source_target_pairs={{0,1},{1,2},{2,3},{4,5},{5,6},{6,7},{8,9},{9,10},{10,11},{12,13},{... | collective-permute-start | bytes 1179656 | tf_op jit(solution)/shard_map/while/body/eval_jaxpr/ppermute | solution.py:20
  147.1 9.6 %all-gather.2 = f32[1,3,12,1024]{3,2,1,0:T(8,128)S(1)} all-gather(f32[1,3,12,128]{3,2,1,0:T(8,128)S(1)} %constant_dynamic-slice_fusion.2), channel_id=2, replica_groups=mesh['mode'=8,'rows'=4] {'mode'}, dimensions={3}, use_global_device_ids=true | all-gather | bytes 165888 | tf_op jit(solution)/shard_map/while/body/eval_jaxpr/all_gather | solution.py:99
  162.1 1.5 pad_maximum_fusion.29
  167.0 1.2 fusion.171
  168.2 1.6 fusion.175
  169.8 1.4 pad_maximum_fusion.30
  177.6 1.3 collective-permute-start
  178.9 5.3 %collective-permute-start.1 = (f32[16,3,2,1024]{3,2,0,1:T(2,128)S(1)}, f32[16,3,2,1024]{3,2,0,1:T(2,128)}, u32[]{:S(2)}, u32[]{:S(2)}) collective-permute-start(f32[16,3,2,1024]{3,2,0,1:T(2,128)S(1)} %get-tuple-element.308), channel_id=1, source_target_pairs={{0,1},{1,2},{2,3},{4,5},{5,6},{6,7},{8,9},{9,10},{10,11},{12,13},{... | collective-permute-start | bytes 1179656 | tf_op jit(solution)/shard_map/while/body/eval_jaxpr/ppermute | solution.py:20
  187.0 8.6 %all-gather.2 = f32[1,3,12,1024]{3,2,1,0:T(8,128)S(1)} all-gather(f32[1,3,12,128]{3,2,1,0:T(8,128)S(1)} %constant_dynamic-slice_fusion.2), channel_id=2, replica_groups=mesh['mode'=8,'rows'=4] {'mode'}, dimensions={3}, use_global_device_ids=true | all-gather | bytes 165888 | tf_op jit(solution)/shard_map/while/body/eval_jaxpr/all_gather | solution.py:99
  201.0 1.5 pad_maximum_fusion.29
  205.9 1.2 fusion.171
  207.1 1.6 fusion.175
  208.7 1.4 pad_maximum_fusion.30
  216.5 1.3 collective-permute-start
  217.8 5.3 %collective-permute-start.1 = (f32[16,3,2,1024]{3,2,0,1:T(2,128)S(1)}, f32[16,3,2,1024]{3,2,0,1:T(2,128)}, u32[]{:S(2)}, u32[]{:S(2)}) collective-permute-start(f32[16,3,2,1024]{3,2,0,1:T(2,128)S(1)} %get-tuple-element.308), channel_id=1, source_target_pairs={{0,1},{1,2},{2,3},{4,5},{5,6},{6,7},{8,9},{9,10},{10,11},{12,13},{... | collective-permute-start | bytes 1179656 | tf_op jit(solution)/shard_map/while/body/eval_jaxpr/ppermute | solution.py:20
  225.8 9.6 %all-gather.2 = f32[1,3,12,1024]{3,2,1,0:T(8,128)S(1)} all-gather(f32[1,3,12,128]{3,2,1,0:T(8,128)S(1)} %constant_dynamic-slice_fusion.2), channel_id=2, replica_groups=mesh['mode'=8,'rows'=4] {'mode'}, dimensions={3}, use_global_device_ids=true | all-gather | bytes 165888 | tf_op jit(solution)/shard_map/while/body/eval_jaxpr/all_gather | solution.py:99
  240.8 1.5 pad_maximum_fusion.29
  246.9 1.6 fusion.175
  248.6 1.4 pad_maximum_fusion.30
  256.3 1.3 collective-permute-start
  257.6 5.3 %collective-permute-start.1 = (f32[16,3,2,1024]{3,2,0,1:T(2,128)S(1)}, f32[16,3,2,1024]{3,2,0,1:T(2,128)}, u32[]{:S(2)}, u32[]{:S(2)}) collective-permute-start(f32[16,3,2,1024]{3,2,0,1:T(2,128)S(1)} %get-tuple-element.308), channel_id=1, source_target_pairs={{0,1},{1,2},{2,3},{4,5},{5,6},{6,7},{8,9},{9,10},{10,11},{12,13},{... | collective-permute-start | bytes 1179656 | tf_op jit(solution)/shard_map/while/body/eval_jaxpr/ppermute | solution.py:20
  265.7 8.6 %all-gather.2 = f32[1,3,12,1024]{3,2,1,0:T(8,128)S(1)} all-gather(f32[1,3,12,128]{3,2,1,0:T(8,128)S(1)} %constant_dynamic-slice_fusion.2), channel_id=2, replica_groups=mesh['mode'=8,'rows'=4] {'mode'}, dimensions={3}, use_global_device_ids=true | all-gather | bytes 165888 | tf_op jit(solution)/shard_map/while/body/eval_jaxpr/all_gather | solution.py:99
  279.7 1.5 pad_maximum_fusion.29
  285.8 1.6 fusion.175
  287.4 1.4 pad_maximum_fusion.30
  295.2 1.3 collective-permute-start
  296.5 5.3 %collective-permute-start.1 = (f32[16,3,2,1024]{3,2,0,1:T(2,128)S(1)}, f32[16,3,2,1024]{3,2,0,1:T(2,128)}, u32[]{:S(2)}, u32[]{:S(2)}) collective-permute-start(f32[16,3,2,1024]{3,2,0,1:T(2,128)S(1)} %get-tuple-element.308), channel_id=1, source_target_pairs={{0,1},{1,2},{2,3},{4,5},{5,6},{6,7},{8,9},{9,10},{10,11},{12,13},{... | collective-permute-start | bytes 1179656 | tf_op jit(solution)/shard_map/while/body/eval_jaxpr/ppermute | solution.py:20
  304.6 9.6 %all-gather.2 = f32[1,3,12,1024]{3,2,1,0:T(8,128)S(1)} all-gather(f32[1,3,12,128]{3,2,1,0:T(8,128)S(1)} %constant_dynamic-slice_fusion.2), channel_id=2, replica_groups=mesh['mode'=8,'rows'=4] {'mode'}, dimensions={3}, use_global_device_ids=true | all-gather | bytes 165888 | tf_op jit(solution)/shard_map/while/body/eval_jaxpr/all_gather | solution.py:99
  319.6 1.5 pad_maximum_fusion.29
  325.7 1.6 fusion.175
  327.3 1.4 pad_maximum_fusion.30
  340.6 3.6 all-to-all-start
  344.2 20.9 %all-to-all-done = f32[8,16,3,8,128]{4,3,2,1,0:T(8,128)S(1)} async-done(((f32[8,16,3,8,128]{4,3,2,1,0:T(8,128)}), f32[8,16,3,8,128]{4,3,2,1,0:T(8,128)S(1)}, u32[]{:S(2)}, u32[]{:S(2)}) %all-to-all-start) | async-done | bytes 1572896 | tf_op jit(solution)/shard_map/all_to_all | solution.py:110
  366.2 1.5 fusion.85
  367.7 2.1 copy.14
  (508 shorter events, 137.2 us)
Async XLA Ops:
  1.0 17.8 %collective-permute-start.4 = (f32[8,3,2,128]{3,2,1,0:T(2,128)S(1)}, f32[8,3,2,128]{3,2,1,0:T(2,128)S(1)}, u32[]{:S(2)}, u32[]{:S(2)}) collective-permute-start(f32[8,3,2,128]{3,2,1,0:T(2,128)S(1)} %get-tuple-element.196), channel_id=1, source_target_pairs={{0,1},{1,2},{2,3},{4,5},{5,6},{6,7},{8,9},{9,10},{10,11},{12,13},{... | collective-permute-start | bytes 73736 | tf_op jit(solution)/shard_map/ppermute | solution.py:20
  6.0 12.8 %collective-permute-start.5 = (f32[8,3,2,128]{3,2,1,0:T(2,128)S(1)}, f32[8,3,2,128]{3,2,1,0:T(2,128)S(1)}, u32[]{:S(2)}, u32[]{:S(2)}) collective-permute-start(f32[8,3,2,128]{3,2,1,0:T(2,128)S(1)} %get-tuple-element.197), channel_id=1, source_target_pairs={{1,0},{2,1},{3,2},{5,4},{6,5},{7,6},{9,8},{10,9},{11,10},{13,12},{... | collective-permute-start | bytes 73736 | tf_op jit(solution)/shard_map/ppermute | solution.py:22
  8.0 7.5 %collective-permute-start.2 = (f32[1,1,2,1024]{3,2,1,0:T(2,128)S(1)}, f32[1,1,2,1024]{3,2,1,0:T(2,128)S(1)}, u32[]{:S(2)}, u32[]{:S(2)}) collective-permute-start(f32[1,1,2,1024]{3,2,1,0:T(2,128)S(1)} %get-tuple-element.198), channel_id=1, source_target_pairs={{0,1},{1,2},{2,3},{4,5},{5,6},{6,7},{8,9},{9,10},{10,11},{12,13},{... | collective-permute-start | bytes 24584 | tf_op jit(solution)/shard_map/ppermute | solution.py:20
  12.6 5.5 %collective-permute-start.3 = (f32[1,1,2,1024]{3,2,1,0:T(2,128)S(1)}, f32[1,1,2,1024]{3,2,1,0:T(2,128)S(1)}, u32[]{:S(2)}, u32[]{:S(2)}) collective-permute-start(f32[1,1,2,1024]{3,2,1,0:T(2,128)S(1)} %get-tuple-element.199), channel_id=1, source_target_pairs={{1,0},{2,1},{3,2},{5,4},{6,5},{7,6},{9,8},{10,9},{11,10},{13,12},{... | collective-permute-start | bytes 24584 | tf_op jit(solution)/shard_map/ppermute | solution.py:22
  13.9 4.9 %copy-start.8 = (f32[8,3,8,128]{3,2,1,0:T(8,128)S(1)}, f32[8,3,8,128]{3,2,1,0:T(8,128)}, u32[]{:S(2)}) copy-start(f32[8,3,8,128]{3,2,1,0:T(8,128)} %param.8) | copy-start | bytes 294916
  13.9 4.9 %copy-start.10 = (s32[8]{0:T(128)S(1)}, s32[8]{0:T(128)}, u32[]{:S(2)}) copy-start(s32[8]{0:T(128)} %param.9) | copy-start | bytes 100
  18.9 20.7 %copy-start.6 = (f32[8,3,12,128]{3,2,1,0:T(8,128)}, f32[8,3,12,128]{3,2,1,0:T(8,128)S(1)}, u32[]{:S(2)}) copy-start(f32[8,3,12,128]{3,2,1,0:T(8,128)S(1)} %get-tuple-element.401) | copy-start | bytes 442372 | tf_op jit(solution)/shard_map/while
  19.2 24.3 %collective-permute-start = (f32[16,3,2,1024]{3,2,0,1:T(2,128)S(1)}, f32[16,3,2,1024]{3,2,0,1:T(2,128)S(1)}, u32[]{:S(2)}, u32[]{:S(2)}) collective-permute-start(f32[16,3,2,1024]{3,2,0,1:T(2,128)S(1)} %get-tuple-element.307), channel_id=1, source_target_pairs={{1,0},{2,1},{3,2},{5,4},{6,5},{7,6},{9,8},{10,9},{11,10},{13,12},{... | collective-permute-start | bytes 1179656 | tf_op jit(solution)/shard_map/while/body/eval_jaxpr/ppermute | solution.py:22
  20.5 23.1 %collective-permute-start.1 = (f32[16,3,2,1024]{3,2,0,1:T(2,128)S(1)}, f32[16,3,2,1024]{3,2,0,1:T(2,128)}, u32[]{:S(2)}, u32[]{:S(2)}) collective-permute-start(f32[16,3,2,1024]{3,2,0,1:T(2,128)S(1)} %get-tuple-element.308), channel_id=1, source_target_pairs={{0,1},{1,2},{2,3},{4,5},{5,6},{6,7},{8,9},{9,10},{10,11},{12,13},{... | collective-permute-start | bytes 1179656 | tf_op jit(solution)/shard_map/while/body/eval_jaxpr/ppermute | solution.py:20
  38.1 3.8 %copy-start.2 = (f32[12,1024]{1,0:T(8,128)S(1)}, f32[12,1024]{1,0:T(8,128)}, u32[]{:S(2)}) copy-start(f32[12,1024]{1,0:T(8,128)} %get-tuple-element.399) | copy-start | bytes 147460 | tf_op jit(solution)/shard_map/while
  43.5 1.6 copy-start.1
  57.7 1.0 copy-start.7
  57.7 1.0 copy-start.11
  58.7 20.6 %copy-start.6 = (f32[8,3,12,128]{3,2,1,0:T(8,128)}, f32[8,3,12,128]{3,2,1,0:T(8,128)S(1)}, u32[]{:S(2)}) copy-start(f32[8,3,12,128]{3,2,1,0:T(8,128)S(1)} %get-tuple-element.401) | copy-start | bytes 442372 | tf_op jit(solution)/shard_map/while
  59.0 24.3 %collective-permute-start = (f32[16,3,2,1024]{3,2,0,1:T(2,128)S(1)}, f32[16,3,2,1024]{3,2,0,1:T(2,128)S(1)}, u32[]{:S(2)}, u32[]{:S(2)}) collective-permute-start(f32[16,3,2,1024]{3,2,0,1:T(2,128)S(1)} %get-tuple-element.307), channel_id=1, source_target_pairs={{1,0},{2,1},{3,2},{5,4},{6,5},{7,6},{9,8},{10,9},{11,10},{13,12},{... | collective-permute-start | bytes 1179656 | tf_op jit(solution)/shard_map/while/body/eval_jaxpr/ppermute | solution.py:22
  60.3 23.0 %collective-permute-start.1 = (f32[16,3,2,1024]{3,2,0,1:T(2,128)S(1)}, f32[16,3,2,1024]{3,2,0,1:T(2,128)}, u32[]{:S(2)}, u32[]{:S(2)}) collective-permute-start(f32[16,3,2,1024]{3,2,0,1:T(2,128)S(1)} %get-tuple-element.308), channel_id=1, source_target_pairs={{0,1},{1,2},{2,3},{4,5},{5,6},{6,7},{8,9},{9,10},{10,11},{12,13},{... | collective-permute-start | bytes 1179656 | tf_op jit(solution)/shard_map/while/body/eval_jaxpr/ppermute | solution.py:20
  77.9 3.8 %copy-start.2 = (f32[12,1024]{1,0:T(8,128)S(1)}, f32[12,1024]{1,0:T(8,128)}, u32[]{:S(2)}) copy-start(f32[12,1024]{1,0:T(8,128)} %get-tuple-element.399) | copy-start | bytes 147460 | tf_op jit(solution)/shard_map/while
  83.3 1.6 copy-start.1
  97.5 1.0 copy-start.7
  97.5 1.0 copy-start.11
  98.6 19.7 %copy-start.6 = (f32[8,3,12,128]{3,2,1,0:T(8,128)}, f32[8,3,12,128]{3,2,1,0:T(8,128)S(1)}, u32[]{:S(2)}) copy-start(f32[8,3,12,128]{3,2,1,0:T(8,128)S(1)} %get-tuple-element.401) | copy-start | bytes 442372 | tf_op jit(solution)/shard_map/while
  98.9 23.4 %collective-permute-start = (f32[16,3,2,1024]{3,2,0,1:T(2,128)S(1)}, f32[16,3,2,1024]{3,2,0,1:T(2,128)S(1)}, u32[]{:S(2)}, u32[]{:S(2)}) collective-permute-start(f32[16,3,2,1024]{3,2,0,1:T(2,128)S(1)} %get-tuple-element.307), channel_id=1, source_target_pairs={{1,0},{2,1},{3,2},{5,4},{6,5},{7,6},{9,8},{10,9},{11,10},{13,12},{... | collective-permute-start | bytes 1179656 | tf_op jit(solution)/shard_map/while/body/eval_jaxpr/ppermute | solution.py:22
  100.2 22.1 %collective-permute-start.1 = (f32[16,3,2,1024]{3,2,0,1:T(2,128)S(1)}, f32[16,3,2,1024]{3,2,0,1:T(2,128)}, u32[]{:S(2)}, u32[]{:S(2)}) collective-permute-start(f32[16,3,2,1024]{3,2,0,1:T(2,128)S(1)} %get-tuple-element.308), channel_id=1, source_target_pairs={{0,1},{1,2},{2,3},{4,5},{5,6},{6,7},{8,9},{9,10},{10,11},{12,13},{... | collective-permute-start | bytes 1179656 | tf_op jit(solution)/shard_map/while/body/eval_jaxpr/ppermute | solution.py:20
  116.8 3.8 %copy-start.2 = (f32[12,1024]{1,0:T(8,128)S(1)}, f32[12,1024]{1,0:T(8,128)}, u32[]{:S(2)}) copy-start(f32[12,1024]{1,0:T(8,128)} %get-tuple-element.399) | copy-start | bytes 147460 | tf_op jit(solution)/shard_map/while
  122.2 1.6 copy-start.1
  136.4 1.0 copy-start.7
  136.4 1.0 copy-start.11
  137.5 20.6 %copy-start.6 = (f32[8,3,12,128]{3,2,1,0:T(8,128)}, f32[8,3,12,128]{3,2,1,0:T(8,128)S(1)}, u32[]{:S(2)}) copy-start(f32[8,3,12,128]{3,2,1,0:T(8,128)S(1)} %get-tuple-element.401) | copy-start | bytes 442372 | tf_op jit(solution)/shard_map/while
  137.8 24.3 %collective-permute-start = (f32[16,3,2,1024]{3,2,0,1:T(2,128)S(1)}, f32[16,3,2,1024]{3,2,0,1:T(2,128)S(1)}, u32[]{:S(2)}, u32[]{:S(2)}) collective-permute-start(f32[16,3,2,1024]{3,2,0,1:T(2,128)S(1)} %get-tuple-element.307), channel_id=1, source_target_pairs={{1,0},{2,1},{3,2},{5,4},{6,5},{7,6},{9,8},{10,9},{11,10},{13,12},{... | collective-permute-start | bytes 1179656 | tf_op jit(solution)/shard_map/while/body/eval_jaxpr/ppermute | solution.py:22
  139.1 23.0 %collective-permute-start.1 = (f32[16,3,2,1024]{3,2,0,1:T(2,128)S(1)}, f32[16,3,2,1024]{3,2,0,1:T(2,128)}, u32[]{:S(2)}, u32[]{:S(2)}) collective-permute-start(f32[16,3,2,1024]{3,2,0,1:T(2,128)S(1)} %get-tuple-element.308), channel_id=1, source_target_pairs={{0,1},{1,2},{2,3},{4,5},{5,6},{6,7},{8,9},{9,10},{10,11},{12,13},{... | collective-permute-start | bytes 1179656 | tf_op jit(solution)/shard_map/while/body/eval_jaxpr/ppermute | solution.py:20
  156.7 3.8 %copy-start.2 = (f32[12,1024]{1,0:T(8,128)S(1)}, f32[12,1024]{1,0:T(8,128)}, u32[]{:S(2)}) copy-start(f32[12,1024]{1,0:T(8,128)} %get-tuple-element.399) | copy-start | bytes 147460 | tf_op jit(solution)/shard_map/while
  162.1 1.6 copy-start.1
  176.3 1.0 copy-start.7
  176.3 1.0 copy-start.11
  177.3 19.7 %copy-start.6 = (f32[8,3,12,128]{3,2,1,0:T(8,128)}, f32[8,3,12,128]{3,2,1,0:T(8,128)S(1)}, u32[]{:S(2)}) copy-start(f32[8,3,12,128]{3,2,1,0:T(8,128)S(1)} %get-tuple-element.401) | copy-start | bytes 442372 | tf_op jit(solution)/shard_map/while
  177.6 23.4 %collective-permute-start = (f32[16,3,2,1024]{3,2,0,1:T(2,128)S(1)}, f32[16,3,2,1024]{3,2,0,1:T(2,128)S(1)}, u32[]{:S(2)}, u32[]{:S(2)}) collective-permute-start(f32[16,3,2,1024]{3,2,0,1:T(2,128)S(1)} %get-tuple-element.307), channel_id=1, source_target_pairs={{1,0},{2,1},{3,2},{5,4},{6,5},{7,6},{9,8},{10,9},{11,10},{13,12},{... | collective-permute-start | bytes 1179656 | tf_op jit(solution)/shard_map/while/body/eval_jaxpr/ppermute | solution.py:22
  178.9 22.1 %collective-permute-start.1 = (f32[16,3,2,1024]{3,2,0,1:T(2,128)S(1)}, f32[16,3,2,1024]{3,2,0,1:T(2,128)}, u32[]{:S(2)}, u32[]{:S(2)}) collective-permute-start(f32[16,3,2,1024]{3,2,0,1:T(2,128)S(1)} %get-tuple-element.308), channel_id=1, source_target_pairs={{0,1},{1,2},{2,3},{4,5},{5,6},{6,7},{8,9},{9,10},{10,11},{12,13},{... | collective-permute-start | bytes 1179656 | tf_op jit(solution)/shard_map/while/body/eval_jaxpr/ppermute | solution.py:20
  195.6 3.8 %copy-start.2 = (f32[12,1024]{1,0:T(8,128)S(1)}, f32[12,1024]{1,0:T(8,128)}, u32[]{:S(2)}) copy-start(f32[12,1024]{1,0:T(8,128)} %get-tuple-element.399) | copy-start | bytes 147460 | tf_op jit(solution)/shard_map/while
  201.0 1.6 copy-start.1
  215.2 1.0 copy-start.7
  215.2 1.0 copy-start.11
  216.2 20.6 %copy-start.6 = (f32[8,3,12,128]{3,2,1,0:T(8,128)}, f32[8,3,12,128]{3,2,1,0:T(8,128)S(1)}, u32[]{:S(2)}) copy-start(f32[8,3,12,128]{3,2,1,0:T(8,128)S(1)} %get-tuple-element.401) | copy-start | bytes 442372 | tf_op jit(solution)/shard_map/while
  216.5 24.3 %collective-permute-start = (f32[16,3,2,1024]{3,2,0,1:T(2,128)S(1)}, f32[16,3,2,1024]{3,2,0,1:T(2,128)S(1)}, u32[]{:S(2)}, u32[]{:S(2)}) collective-permute-start(f32[16,3,2,1024]{3,2,0,1:T(2,128)S(1)} %get-tuple-element.307), channel_id=1, source_target_pairs={{1,0},{2,1},{3,2},{5,4},{6,5},{7,6},{9,8},{10,9},{11,10},{13,12},{... | collective-permute-start | bytes 1179656 | tf_op jit(solution)/shard_map/while/body/eval_jaxpr/ppermute | solution.py:22
  217.8 23.0 %collective-permute-start.1 = (f32[16,3,2,1024]{3,2,0,1:T(2,128)S(1)}, f32[16,3,2,1024]{3,2,0,1:T(2,128)}, u32[]{:S(2)}, u32[]{:S(2)}) collective-permute-start(f32[16,3,2,1024]{3,2,0,1:T(2,128)S(1)} %get-tuple-element.308), channel_id=1, source_target_pairs={{0,1},{1,2},{2,3},{4,5},{5,6},{6,7},{8,9},{9,10},{10,11},{12,13},{... | collective-permute-start | bytes 1179656 | tf_op jit(solution)/shard_map/while/body/eval_jaxpr/ppermute | solution.py:20
  235.4 3.8 %copy-start.2 = (f32[12,1024]{1,0:T(8,128)S(1)}, f32[12,1024]{1,0:T(8,128)}, u32[]{:S(2)}) copy-start(f32[12,1024]{1,0:T(8,128)} %get-tuple-element.399) | copy-start | bytes 147460 | tf_op jit(solution)/shard_map/while
  240.8 1.6 copy-start.1
  255.0 1.0 copy-start.7
  255.0 1.0 copy-start.11
  256.0 19.7 %copy-start.6 = (f32[8,3,12,128]{3,2,1,0:T(8,128)}, f32[8,3,12,128]{3,2,1,0:T(8,128)S(1)}, u32[]{:S(2)}) copy-start(f32[8,3,12,128]{3,2,1,0:T(8,128)S(1)} %get-tuple-element.401) | copy-start | bytes 442372 | tf_op jit(solution)/shard_map/while
  256.3 23.4 %collective-permute-start = (f32[16,3,2,1024]{3,2,0,1:T(2,128)S(1)}, f32[16,3,2,1024]{3,2,0,1:T(2,128)S(1)}, u32[]{:S(2)}, u32[]{:S(2)}) collective-permute-start(f32[16,3,2,1024]{3,2,0,1:T(2,128)S(1)} %get-tuple-element.307), channel_id=1, source_target_pairs={{1,0},{2,1},{3,2},{5,4},{6,5},{7,6},{9,8},{10,9},{11,10},{13,12},{... | collective-permute-start | bytes 1179656 | tf_op jit(solution)/shard_map/while/body/eval_jaxpr/ppermute | solution.py:22
  257.6 22.1 %collective-permute-start.1 = (f32[16,3,2,1024]{3,2,0,1:T(2,128)S(1)}, f32[16,3,2,1024]{3,2,0,1:T(2,128)}, u32[]{:S(2)}, u32[]{:S(2)}) collective-permute-start(f32[16,3,2,1024]{3,2,0,1:T(2,128)S(1)} %get-tuple-element.308), channel_id=1, source_target_pairs={{0,1},{1,2},{2,3},{4,5},{5,6},{6,7},{8,9},{9,10},{10,11},{12,13},{... | collective-permute-start | bytes 1179656 | tf_op jit(solution)/shard_map/while/body/eval_jaxpr/ppermute | solution.py:20
  274.3 3.8 %copy-start.2 = (f32[12,1024]{1,0:T(8,128)S(1)}, f32[12,1024]{1,0:T(8,128)}, u32[]{:S(2)}) copy-start(f32[12,1024]{1,0:T(8,128)} %get-tuple-element.399) | copy-start | bytes 147460 | tf_op jit(solution)/shard_map/while
  279.7 1.6 copy-start.1
  293.9 1.0 copy-start.7
  293.9 1.0 copy-start.11
  294.9 20.6 %copy-start.6 = (f32[8,3,12,128]{3,2,1,0:T(8,128)}, f32[8,3,12,128]{3,2,1,0:T(8,128)S(1)}, u32[]{:S(2)}) copy-start(f32[8,3,12,128]{3,2,1,0:T(8,128)S(1)} %get-tuple-element.401) | copy-start | bytes 442372 | tf_op jit(solution)/shard_map/while
  295.2 24.3 %collective-permute-start = (f32[16,3,2,1024]{3,2,0,1:T(2,128)S(1)}, f32[16,3,2,1024]{3,2,0,1:T(2,128)S(1)}, u32[]{:S(2)}, u32[]{:S(2)}) collective-permute-start(f32[16,3,2,1024]{3,2,0,1:T(2,128)S(1)} %get-tuple-element.307), channel_id=1, source_target_pairs={{1,0},{2,1},{3,2},{5,4},{6,5},{7,6},{9,8},{10,9},{11,10},{13,12},{... | collective-permute-start | bytes 1179656 | tf_op jit(solution)/shard_map/while/body/eval_jaxpr/ppermute | solution.py:22
  296.5 23.0 %collective-permute-start.1 = (f32[16,3,2,1024]{3,2,0,1:T(2,128)S(1)}, f32[16,3,2,1024]{3,2,0,1:T(2,128)}, u32[]{:S(2)}, u32[]{:S(2)}) collective-permute-start(f32[16,3,2,1024]{3,2,0,1:T(2,128)S(1)} %get-tuple-element.308), channel_id=1, source_target_pairs={{0,1},{1,2},{2,3},{4,5},{5,6},{6,7},{8,9},{9,10},{10,11},{12,13},{... | collective-permute-start | bytes 1179656 | tf_op jit(solution)/shard_map/while/body/eval_jaxpr/ppermute | solution.py:20
  314.1 3.8 %copy-start.2 = (f32[12,1024]{1,0:T(8,128)S(1)}, f32[12,1024]{1,0:T(8,128)}, u32[]{:S(2)}) copy-start(f32[12,1024]{1,0:T(8,128)} %get-tuple-element.399) | copy-start | bytes 147460 | tf_op jit(solution)/shard_map/while
  319.5 1.6 copy-start.1
  333.7 1.0 copy-start.7
  333.7 1.0 copy-start.11
  340.6 24.5 %all-to-all-start = ((f32[8,16,3,8,128]{4,3,2,1,0:T(8,128)}), f32[8,16,3,8,128]{4,3,2,1,0:T(8,128)S(1)}, u32[]{:S(2)}, u32[]{:S(2)}) async-start(f32[8,16,3,8,128]{4,3,2,1,0:T(8,128)} %bitcast_dynamic-update-slice_fusion), calls=%async_computation | async-start | bytes 3145728 | tf_op jit(solution)/shard_map/all_to_all | solution.py:110
  365.3 0.8 copy-start.9
  (32 other events, 25.4 us)
